TPU v7x, 32 devices: a whole 2x2x4 slice. The times are simulated.
32 devices in a mesh: row: 4 (over y, core), col: 8 (over z, x).
Axes of the slice: x: 2, y: 2, z: 4, core: 2. Of those that a mesh axis runs over, the one named last changes fastest.
Arguments:
- kernel: float32 [4, 4, 256, 2, 8, 256], P(None, 'row', None, None, 'col'), may hold values from -40 to 40, as said below
Outputs:
- trailing: float32 [4, 4, 256, 2, 8, 256], P(None, 'row', None, None, 'col')
- panels: float32 [4, 4, 256, 3, 256], P(None, 'row')
Inputs may be any that keep to these rules, and one draw needn't show every extreme that they name: kernel is symmetric and positive definite with smallest eigenvalue at least 1.
All inputs are finite; a program needn't handle non-finite values.
Results may differ from a plain program's by a relative error of at most 0.0003.
Values sent between devices are 32-bit elements; how exact they have to be, the bound alone decides.
A program may use at most 128 MiB of HBM per device.

v0:
```python
import jax
import jax.numpy as jnp
from jax import lax
from jax.sharding import PartitionSpec as P

STEPS = 3


def broadcast(value, axis, source):
    kept = jnp.where(lax.axis_index(axis) == source, value, 0).astype(value.dtype)
    return lax.psum(kept, axis)


def shards(kernel):
    row_tiles, _, tile_size, col_tiles, _, _ = kernel.shape
    row_count = lax.axis_size("row")
    col_count = lax.axis_size("col")
    row_index = lax.axis_index("row")
    col_index = lax.axis_index("col")
    stride = col_count // row_count
    working = kernel.reshape(row_tiles, tile_size, col_tiles, tile_size)
    identity = jnp.eye(tile_size, dtype=jnp.float32)
    tile_rows = jnp.arange(row_tiles) * row_count + row_index
    tile_cols = jnp.arange(col_tiles) * col_count + col_index
    collected = []
    for panel_step in range(STEPS):
        local_row = panel_step // row_count
        local_col = panel_step // col_count
        column_slab = working[:, :, local_col, :]
        diagonal = broadcast(column_slab[local_row], "row", panel_step % row_count)
        factor = jnp.linalg.cholesky(diagonal)
        inverse = lax.linalg.triangular_solve(factor, identity, left_side=True, lower=True)
        panel = jnp.einsum("art,st->ars", column_slab, inverse, precision=lax.Precision.HIGHEST)
        panel = jnp.where((tile_rows >= panel_step)[:, None, None], panel, jnp.float32(0.0))
        my_panel = broadcast(panel, "col", panel_step % col_count)
        collected.append(my_panel)
        selected = lax.dynamic_index_in_dim(
            my_panel.reshape(col_tiles, stride, tile_size, tile_size),
            col_index // row_count,
            1,
            keepdims=False,
        )
        gathered = lax.all_gather(selected, "row", axis=0, tiled=True)
        col_panel = lax.dynamic_index_in_dim(
            gathered.reshape(row_count, col_tiles, tile_size, tile_size),
            col_index % row_count,
            0,
            keepdims=False,
        )
        row_terms = jnp.where((tile_rows > panel_step)[:, None, None], my_panel, jnp.float32(0.0))
        col_terms = jnp.where((tile_cols > panel_step)[:, None, None], col_panel, jnp.float32(0.0))
        correction = jnp.einsum(
            "art,cst->arcs", row_terms, col_terms, precision=lax.Precision.HIGHEST
        )
        keep_mask = (tile_rows > panel_step)[:, None, None, None] & (tile_cols > panel_step)[
            None, None, :, None
        ]
        working = jnp.where(keep_mask, working - correction, jnp.float32(0.0))
    trailing = working.reshape(kernel.shape)
    panels = jnp.stack(collected, axis=2).reshape(row_tiles, 1, tile_size, STEPS, tile_size)
    return (trailing, panels)


def solution(mesh):
    in_specs = (P(None, "row", None, None, "col", None),)
    out_specs = (P(None, "row", None, None, "col", None), P(None, "row", None, None, None))
    return jax.shard_map(shards, mesh=mesh, in_specs=in_specs, out_specs=out_specs, check_vma=False)
```

profile of v0, /device:TPU:0, one launch (start us, length us, event | category | flops | bytes accessed | tf_op | source)
XLA Modules:
  0.0 669.3 jit_solution(3093933253821480764)
XLA Ops:
  7.2 4.6 copy.23
  12.7 35.0 %all-reduce.8.cloned.1.call-done = f32[256,256]{0,1:T(8,128)} async-done(((f32[256,256]{0,1:T(8,128)}), f32[256,256]{0,1:T(8,128)}) %all-reduce.8.cloned.1.call-update) | async-done | bytes 262160 | tf_op jit(solution)/shard_map/psum | solution.py:11
  49.8 11.7 %cholesky.172 = f32[128,128]{1,0:T(8,128)S(1)} custom-call(f32[128,128]{1,0:T(8,128)S(1)} %cholesky.270), custom_call_target="Cholesky" | custom-call | tf_op jit(solution)/shard_map/jit(cholesky)/cholesky | solution.py:31
  61.5 9.8 %custom-call.15 = f32[1,128,128]{1,2,0:T(8,128)S(1)} custom-call(f32[1,128,128]{2,1,0:T(8,128)S(1)} %get-tuple-element.72), custom_call_target="InvertDiagBlocksLowerTriangular" | custom-call | tf_op jit(solution)/shard_map/jit(cholesky)/cholesky | solution.py:31
  71.9 11.7 %cholesky.189 = f32[128,128]{1,0:T(8,128)S(1)} custom-call(f32[128,128]{1,0:T(8,128)S(1)} %convolution_subtract_fusion.5), custom_call_target="Cholesky" | custom-call | tf_op jit(solution)/shard_map/jit(cholesky)/cholesky | solution.py:31
  85.8 4.6 while.6
  86.9 1.4 bitcast_dynamic-update-slice_fusion.6
  89.0 1.4 bitcast_dynamic-update-slice_fusion.6
  90.4 19.7 %custom-call.16 = f32[2,128,128]{1,2,0:T(8,128)S(1)} custom-call(f32[2,128,128]{2,1,0:T(8,128)S(1)} %get-tuple-element.24), custom_call_target="InvertDiagBlocksLowerTriangular" | custom-call | tf_op jit(solution)/shard_map/triangular_solve/custom-call.0 | solution.py:32
  111.0 2.0 fusion.3
  113.1 78.4 %all-reduce.10.cloned.1.call-done = f32[4,256,256]{1,2,0:T(8,128)} async-done(((f32[4,256,256]{1,2,0:T(8,128)}), f32[4,256,256]{1,2,0:T(8,128)}) %all-reduce.10.cloned.1.call-update) | async-done | bytes 1048592 | tf_op jit(solution)/shard_map/psum | solution.py:11
  191.6 2.0 constant_dynamic-slice_fusion.5
  193.6 2.0 copy.60
  195.8 22.1 %all-gather.7.cloned.1.call-done = f32[8,1,256,256]{3,2,1,0:T(8,128)} async-done(((f32[2,1,256,256]{3,2,1,0:T(8,128)}), f32[8,1,256,256]{3,2,1,0:T(8,128)}) %all-gather.7.cloned.1.call-update) | async-done | bytes 2097168 | tf_op jit(solution)/shard_map/all_gather | solution.py:43
  217.9 3.2 subtract_select_fusion.1
  221.1 1.3 copy-done
  223.4 32.2 %all-reduce.12.cloned.1.call-done = f32[256,256]{0,1:T(8,128)} async-done(((f32[256,256]{0,1:T(8,128)}), f32[256,256]{0,1:T(8,128)}) %all-reduce.12.cloned.1.call-update) | async-done | bytes 262160 | tf_op jit(solution)/shard_map/psum | solution.py:11
  258.4 11.7 %cholesky.206 = f32[128,128]{1,0:T(8,128)S(1)} custom-call(f32[128,128]{1,0:T(8,128)S(1)} %cholesky.273), custom_call_target="Cholesky" | custom-call | tf_op jit(solution)/shard_map/jit(cholesky)/cholesky | solution.py:31
  270.8 10.4 %custom-call.17 = f32[1,128,128]{1,2,0:T(8,128)} custom-call(f32[1,128,128]{2,1,0:T(8,128)S(1)} %get-tuple-element.68), custom_call_target="InvertDiagBlocksLowerTriangular" | custom-call | tf_op jit(solution)/shard_map/jit(cholesky)/cholesky | solution.py:31
  281.9 1.7 constant_dynamic-update-slice_fusion.1
  284.7 11.7 %cholesky.223 = f32[128,128]{1,0:T(8,128)S(1)} custom-call(f32[128,128]{1,0:T(8,128)S(1)} %convolution_subtract_fusion.4), custom_call_target="Cholesky" | custom-call | tf_op jit(solution)/shard_map/jit(cholesky)/cholesky | solution.py:31
  299.8 6.0 while.7
  300.7 2.2 bitcast_dynamic-update-slice_fusion.7
  303.7 2.2 bitcast_dynamic-update-slice_fusion.7
  306.5 20.5 %custom-call.18 = f32[2,128,128]{1,2,0:T(8,128)S(1)} custom-call(f32[2,128,128]{2,1,0:T(8,128)} %copy-done.7), custom_call_target="InvertDiagBlocksLowerTriangular" | custom-call | tf_op jit(solution)/shard_map/triangular_solve/custom-call.0 | solution.py:32
  328.8 2.1 fusion.1
  330.9 78.4 %all-reduce.14.cloned.1.call-done = f32[4,256,256]{1,2,0:T(8,128)} async-done(((f32[4,256,256]{1,2,0:T(8,128)}), f32[4,256,256]{1,2,0:T(8,128)}) %all-reduce.14.cloned.1.call-update) | async-done | bytes 1048592 | tf_op jit(solution)/shard_map/psum | solution.py:11
  411.6 22.2 %all-gather.9.cloned.1.call-done = f32[8,1,256,256]{3,2,1,0:T(8,128)} async-done(((f32[2,1,256,256]{3,2,1,0:T(8,128)}), f32[8,1,256,256]{3,2,1,0:T(8,128)}) %all-gather.9.cloned.1.call-update) | async-done | bytes 2097168 | tf_op jit(solution)/shard_map/all_gather | solution.py:43
  433.8 4.2 subtract_select_fusion
  439.0 32.1 %all-reduce.16.cloned.1.call-done = f32[256,256]{0,1:T(8,128)} async-done(((f32[256,256]{0,1:T(8,128)}), f32[256,256]{0,1:T(8,128)}) %all-reduce.16.cloned.1.call-update) | async-done | bytes 262160 | tf_op jit(solution)/shard_map/psum | solution.py:11
  471.1 1.8 copy.35
  474.7 11.7 %cholesky.240 = f32[128,128]{1,0:T(8,128)S(1)} custom-call(f32[128,128]{1,0:T(8,128)S(1)} %cholesky.276), custom_call_target="Cholesky" | custom-call | tf_op jit(solution)/shard_map/jit(cholesky)/cholesky | solution.py:31
  487.1 10.4 %custom-call.19 = f32[1,128,128]{1,2,0:T(8,128)} custom-call(f32[1,128,128]{2,1,0:T(8,128)S(1)} %get-tuple-element.64), custom_call_target="InvertDiagBlocksLowerTriangular" | custom-call | tf_op jit(solution)/shard_map/jit(cholesky)/cholesky | solution.py:31
  498.2 1.7 constant_dynamic-update-slice_fusion
  501.1 11.7 %cholesky.257 = f32[128,128]{1,0:T(8,128)S(1)} custom-call(f32[128,128]{1,0:T(8,128)S(1)} %convolution_subtract_fusion.3), custom_call_target="Cholesky" | custom-call | tf_op jit(solution)/shard_map/jit(cholesky)/cholesky | solution.py:31
  516.1 6.0 while.8
  517.0 2.3 bitcast_dynamic-update-slice_fusion.8
  519.9 2.2 bitcast_dynamic-update-slice_fusion.8
  522.7 20.5 %custom-call.20 = f32[2,128,128]{1,2,0:T(8,128)S(1)} custom-call(f32[2,128,128]{2,1,0:T(8,128)} %copy-done.6), custom_call_target="InvertDiagBlocksLowerTriangular" | custom-call | tf_op jit(solution)/shard_map/triangular_solve/custom-call.0 | solution.py:32
  545.0 2.1 fusion
  547.1 78.4 %all-reduce.18.cloned.1.call-done = f32[4,256,256]{1,2,0:T(8,128)} async-done(((f32[4,256,256]{1,2,0:T(8,128)}), f32[4,256,256]{1,2,0:T(8,128)}) %all-reduce.18.cloned.1.call-update) | async-done | bytes 1048592 | tf_op jit(solution)/shard_map/psum | solution.py:11
  625.5 1.9 constant_dynamic-slice_fusion.3
  627.4 2.0 copy.62
  629.5 3.4 maximum_bitcast_fusion
  632.9 3.6 copy.42
  636.6 15.2 %all-gather.11.cloned.1.call-done = f32[8,1,256,256]{3,2,1,0:T(8,128)} async-done(((f32[2,1,256,256]{3,2,1,0:T(8,128)}), f32[8,1,256,256]{3,2,1,0:T(8,128)}) %all-gather.11.cloned.1.call-update) | async-done | bytes 2097168 | tf_op jit(solution)/shard_map/all_gather | solution.py:43
  651.7 4.5 select_bitcast_fusion
  656.3 6.0 copy.41
  (106 shorter events, 32.0 us)
Async XLA Ops:
  7.2 40.5 %all-reduce.8.cloned.1.call-start = ((), (), s32[]{:S(2)}) async-start(), calls=%async_computation | async-start | bytes 524288 | tf_op jit(solution)/shard_map/psum | solution.py:11
  12.5 179.0 %all-reduce.10.cloned.1.call-start = ((), (), s32[]{:S(2)}) async-start(), calls=%async_computation.1 | async-start | bytes 2097152 | tf_op jit(solution)/shard_map/psum | solution.py:11
  113.1 104.9 %all-gather.7.cloned.1.call-start = ((), (), s32[]{:S(2)}) async-start(), calls=%async_computation.6 | async-start | bytes 2621440 | tf_op jit(solution)/shard_map/all_gather | solution.py:43
  191.6 26.3 %copy-start.2 = (f32[4,256,256]{1,2,0:T(8,128)S(1)}, f32[4,256,256]{1,2,0:T(8,128)}, u32[]{:S(2)}) copy-start(f32[4,256,256]{1,2,0:T(8,128)} %all-reduce.10.cloned.1.call-done) | copy-start | bytes 3145732
  195.6 60.0 %all-reduce.12.cloned.1.call-start = ((), (), s32[]{:S(2)}) async-start(), calls=%async_computation.2 | async-start | bytes 524288 | tf_op jit(solution)/shard_map/psum | solution.py:11
  221.1 1.3 copy-start
  223.2 186.2 %all-reduce.14.cloned.1.call-start = ((), (), s32[]{:S(2)}) async-start(), calls=%async_computation.3 | async-start | bytes 2097152 | tf_op jit(solution)/shard_map/psum | solution.py:11
  257.7 0.7 copy-start.4
  258.4 70.4 %copy-start.1 = (f32[4,256,2,256]{1,3,2,0:T(8,128)S(1)}, f32[4,256,2,256]{1,3,2,0:T(8,128)}, u32[]{:S(2)}) copy-start(f32[4,256,2,256]{1,3,2,0:T(8,128)} %copy-done) | copy-start | bytes 6291460
  305.9 0.6 copy-start.7
  330.8 102.9 %all-gather.9.cloned.1.call-start = ((), (), s32[]{:S(2)}) async-start(), calls=%async_computation.7 | async-start | bytes 2621440 | tf_op jit(solution)/shard_map/all_gather | solution.py:43
  411.4 59.7 %all-reduce.16.cloned.1.call-start = ((), (), s32[]{:S(2)}) async-start(), calls=%async_computation.4 | async-start | bytes 524288 | tf_op jit(solution)/shard_map/psum | solution.py:11
  438.7 186.8 %all-reduce.18.cloned.1.call-start = ((), (), s32[]{:S(2)}) async-start(), calls=%async_computation.5 | async-start | bytes 2097152 | tf_op jit(solution)/shard_map/psum | solution.py:11
  474.0 0.7 copy-start.5
  522.1 0.7 copy-start.6
  547.1 104.7 %all-gather.11.cloned.1.call-start = ((), (), s32[]{:S(2)}) async-start(), calls=%async_computation.8 | async-start | bytes 2621440 | tf_op jit(solution)/shard_map/all_gather | solution.py:43
  632.9 18.8 %copy-start.3 = (f32[4,256,256]{1,2,0:T(8,128)S(1)}, f32[4,256,256]{1,2,0:T(8,128)}, u32[]{:S(2)}) copy-start(f32[4,256,256]{1,2,0:T(8,128)} %all-reduce.18.cloned.1.call-done) | copy-start | bytes 3145732
Sparse Core Ops, SparseCore 0:
  12.7 34.9 all-reduce.7
  113.2 78.3 all-reduce.9
  195.7 22.1 all-gather.6
  223.3 32.2 all-reduce.11
  331.0 78.3 all-reduce.13
  411.6 22.1 all-gather.8
  438.8 32.2 all-reduce.15
  547.2 78.2 all-reduce.17
  629.5 22.1 all-gather.10
where the time goes:
time: 678 us; the launch traced here: 669 us
  waiting for transfers between devices  394 us (58%)
  other arithmetic  177 us (26%)
  local copies, waits for them, and re-layouts  49.2 us (7%)
  matrix products  28.4 us (4%)
  between operations  18.7 us (3%)
    psum x6, waiting for transfers between devices, broadcast(): return lax.psum(kept, axis)  335 us
    another operation x20, other arithmetic, shards(): factor = jnp.linalg.cholesky(diagonal)  106 us
    another operation x7, other arithmetic, shards(): lax.linalg.triangular_solve(factor, identity, left_side=True, lower=True)  62.2 us
    all_gather x3, waiting for transfers between devices, shards(): gathered = lax.all_gather(selected, 'row', axis=0, tiled=True)  59.5 us
    unnamed x22, local copies, waits for them, and re-layouts  23.3 us
    another operation x22, local copies, waits for them, and re-layouts, shards(): lax.linalg.triangular_solve(factor, identity, left_side=True, lower=True)  15.6 us
  transfers between devices with their start and end apart: 9, of which 9 were waited for; matrix products, arithmetic and copies ran while one was open for 1% of the time, Pallas kernels for 0%

commit v1 on v0

--- a/solution.py
+++ b/solution.py
@@ -4,6 +4,12 @@
 from jax.sharding import PartitionSpec as P
 
 STEPS = 3
+
+
+def laid_out(pieces, dim):
+    shape = list(pieces.shape[1:])
+    shape[dim] *= pieces.shape[0]
+    return jnp.moveaxis(pieces, 0, dim).reshape(shape)
 
 
 def broadcast(value, axis, source):
@@ -40,7 +46,14 @@
             1,
             keepdims=False,
         )
-        gathered = lax.all_gather(selected, "row", axis=0, tiled=True)
+        size = lax.axis_size("row")
+        ahead = [(i, (i + 1) % size) for i in range(size)]
+        blocks = [selected]
+        while len(blocks) < size:
+            blocks.append(lax.ppermute(blocks[-1], "row", ahead))
+        index = lax.axis_index("row")
+        blocks = jnp.stack(blocks)[(index - jnp.arange(size)) % size]
+        gathered = laid_out(blocks, 0)
         col_panel = lax.dynamic_index_in_dim(
             gathered.reshape(row_count, col_tiles, tile_size, tile_size),
             col_index % row_count,

time: 678 us -> 703 us (1.037)
  waiting for transfers between devices: 394 us -> 405 us
    ppermute x0 -> x9, waiting for transfers between devices: none -> 71 us  [shards(): blocks.append(lax.ppermute(blocks[-1], 'row', ahead))]
    all_gather x3 -> x0, waiting for transfers between devices: 59.5 us -> none  [shards(): gathered = lax.all_gather(selected, 'row', axis=0, tiled=True)]
    gather x0 -> x3, local copies, waits for them, and re-layouts: none -> 9.36 us  [shards(): blocks = jnp.stack(blocks)[(index - jnp.arange(size)) % size]]
    unnamed x22 -> x33, local copies, waits for them, and re-layouts: 23.3 us -> 19.8 us
  transfers between devices with their start and end apart: 9 -> 15, of which waited for: 9 -> 15; matrix products, arithmetic and copies ran while one was open for 1% -> 1% of each run, Pallas kernels for 0% -> 0%
where the time goes in v1:
time: 703 us; the launch traced here: 693 us
  waiting for transfers between devices  405 us (58%)
  other arithmetic  184 us (26%)
  local copies, waits for them, and re-layouts  56.2 us (8%)
  matrix products  28.4 us (4%)
  between operations  18.7 us (3%)
    psum x6, waiting for transfers between devices, broadcast(): return lax.psum(kept, axis)  333 us
    another operation x20, other arithmetic, shards(): factor = jnp.linalg.cholesky(diagonal)  106 us
    ppermute x9, waiting for transfers between devices, shards(): blocks.append(lax.ppermute(blocks[-1], 'row', ahead))  71 us
    another operation x7, other arithmetic, shards(): lax.linalg.triangular_solve(factor, identity, left_side=True, lower=True)  62.2 us
    unnamed x33, local copies, waits for them, and re-layouts  19.8 us
    another operation x22, local copies, waits for them, and re-layouts, shards(): lax.linalg.triangular_solve(factor, identity, left_side=True, lower=True)  15.1 us
  transfers between devices with their start and end apart: 15, of which 15 were waited for; matrix products, arithmetic and copies ran while one was open for 1% of the time, Pallas kernels for 0%

profile of v1, /device:TPU:0, one launch (start us, length us, event | category | flops | bytes accessed | tf_op | source)
XLA Modules:
  0.0 693.4 jit_solution(10936073787764377136)
XLA Ops:
  7.2 4.6 copy.20
  12.7 35.1 %all-reduce.8.cloned.1.call-done = f32[256,256]{0,1:T(8,128)} async-done(((f32[256,256]{0,1:T(8,128)}), f32[256,256]{0,1:T(8,128)}) %all-reduce.8.cloned.1.call-update) | async-done | bytes 262160 | tf_op jit(solution)/shard_map/psum | solution.py:17
  49.8 11.7 %cholesky.172 = f32[128,128]{1,0:T(8,128)S(1)} custom-call(f32[128,128]{1,0:T(8,128)S(1)} %cholesky.270), custom_call_target="Cholesky" | custom-call | tf_op jit(solution)/shard_map/jit(cholesky)/cholesky | solution.py:37
  61.5 9.8 %custom-call.15 = f32[1,128,128]{1,2,0:T(8,128)S(1)} custom-call(f32[1,128,128]{2,1,0:T(8,128)S(1)} %get-tuple-element.72), custom_call_target="InvertDiagBlocksLowerTriangular" | custom-call | tf_op jit(solution)/shard_map/jit(cholesky)/cholesky | solution.py:37
  71.9 11.7 %cholesky.189 = f32[128,128]{1,0:T(8,128)S(1)} custom-call(f32[128,128]{1,0:T(8,128)S(1)} %convolution_subtract_fusion.5), custom_call_target="Cholesky" | custom-call | tf_op jit(solution)/shard_map/jit(cholesky)/cholesky | solution.py:37
  85.7 4.1 while.6
  89.8 19.7 %custom-call.16 = f32[2,128,128]{1,2,0:T(8,128)S(1)} custom-call(f32[2,128,128]{2,1,0:T(8,128)S(1)} %get-tuple-element.24), custom_call_target="InvertDiagBlocksLowerTriangular" | custom-call | tf_op jit(solution)/shard_map/triangular_solve/custom-call.0 | solution.py:38
  110.4 2.0 fusion.3
  112.5 78.3 %all-reduce.10.cloned.1.call-done = f32[4,256,256]{1,2,0:T(8,128)} async-done(((f32[4,256,256]{1,2,0:T(8,128)}), f32[4,256,256]{1,2,0:T(8,128)}) %all-reduce.10.cloned.1.call-update) | async-done | bytes 1048592 | tf_op jit(solution)/shard_map/psum | solution.py:17
  192.2 8.6 %collective-permute-done = f32[2,256,256]{2,1,0:T(8,128)S(1)} collective-permute-done((f32[2,256,256]{2,1,0:T(8,128)S(1)}, f32[2,256,256]{2,1,0:T(8,128)S(1)}, u32[]{:S(2)}, u32[]{:S(2)}) %collective-permute-start) | collective-permute-done | bytes 524320 | tf_op jit(solution)/shard_map/ppermute | solution.py:53
  200.8 8.7 %collective-permute-done.1 = f32[2,256,256]{2,1,0:T(8,128)} collective-permute-done((f32[2,256,256]{2,1,0:T(8,128)S(1)}, f32[2,256,256]{2,1,0:T(8,128)}, u32[]{:S(2)}, u32[]{:S(2)}) %collective-permute-start.1) | collective-permute-done | bytes 524320 | tf_op jit(solution)/shard_map/ppermute | solution.py:53
  209.6 8.7 %collective-permute-done.2 = f32[2,256,256]{2,1,0:T(8,128)S(1)} collective-permute-done((f32[2,256,256]{2,1,0:T(8,128)}, f32[2,256,256]{2,1,0:T(8,128)S(1)}, u32[]{:S(2)}, u32[]{:S(2)}) %collective-permute-start.2) | collective-permute-done | bytes 524320 | tf_op jit(solution)/shard_map/ppermute | solution.py:53
  218.3 2.5 pad_maximum_fusion
  220.8 3.7 gather_fusion
  224.5 3.2 subtract_select_fusion.1
  230.0 31.8 %all-reduce.12.cloned.1.call-done = f32[256,256]{0,1:T(8,128)} async-done(((f32[256,256]{0,1:T(8,128)}), f32[256,256]{0,1:T(8,128)}) %all-reduce.12.cloned.1.call-update) | async-done | bytes 262160 | tf_op jit(solution)/shard_map/psum | solution.py:17
  264.6 11.7 %cholesky.206 = f32[128,128]{1,0:T(8,128)S(1)} custom-call(f32[128,128]{1,0:T(8,128)S(1)} %cholesky.273), custom_call_target="Cholesky" | custom-call | tf_op jit(solution)/shard_map/jit(cholesky)/cholesky | solution.py:37
  277.1 10.4 %custom-call.17 = f32[1,128,128]{1,2,0:T(8,128)} custom-call(f32[1,128,128]{2,1,0:T(8,128)S(1)} %get-tuple-element.68), custom_call_target="InvertDiagBlocksLowerTriangular" | custom-call | tf_op jit(solution)/shard_map/jit(cholesky)/cholesky | solution.py:37
  291.0 11.7 %cholesky.223 = f32[128,128]{1,0:T(8,128)S(1)} custom-call(f32[128,128]{1,0:T(8,128)S(1)} %convolution_subtract_fusion.4), custom_call_target="Cholesky" | custom-call | tf_op jit(solution)/shard_map/jit(cholesky)/cholesky | solution.py:37
  306.1 5.8 while.7
  307.0 2.2 bitcast_dynamic-update-slice_fusion.7
  309.8 2.1 bitcast_dynamic-update-slice_fusion.7
  312.5 20.5 %custom-call.18 = f32[2,128,128]{1,2,0:T(8,128)S(1)} custom-call(f32[2,128,128]{2,1,0:T(8,128)} %copy-done.14), custom_call_target="InvertDiagBlocksLowerTriangular" | custom-call | tf_op jit(solution)/shard_map/triangular_solve/custom-call.0 | solution.py:38
  334.8 2.1 fusion.1
  336.9 78.4 %all-reduce.14.cloned.1.call-done = f32[4,256,256]{1,2,0:T(8,128)} async-done(((f32[4,256,256]{1,2,0:T(8,128)}), f32[4,256,256]{1,2,0:T(8,128)}) %all-reduce.14.cloned.1.call-update) | async-done | bytes 1048592 | tf_op jit(solution)/shard_map/psum | solution.py:17
  416.6 8.6 %collective-permute-done.3 = f32[2,256,256]{2,1,0:T(8,128)S(1)} collective-permute-done((f32[2,256,256]{2,1,0:T(8,128)S(1)}, f32[2,256,256]{2,1,0:T(8,128)S(1)}, u32[]{:S(2)}, u32[]{:S(2)}) %collective-permute-start.3) | collective-permute-done | bytes 524320 | tf_op jit(solution)/shard_map/ppermute | solution.py:53
  425.2 8.6 %collective-permute-done.4 = f32[2,256,256]{2,1,0:T(8,128)S(1)} collective-permute-done((f32[2,256,256]{2,1,0:T(8,128)S(1)}, f32[2,256,256]{2,1,0:T(8,128)S(1)}, u32[]{:S(2)}, u32[]{:S(2)}) %collective-permute-start.4) | collective-permute-done | bytes 524320 | tf_op jit(solution)/shard_map/ppermute | solution.py:53
  433.9 8.5 %collective-permute-done.5 = f32[2,256,256]{2,1,0:T(8,128)S(1)} collective-permute-done((f32[2,256,256]{2,1,0:T(8,128)S(1)}, f32[2,256,256]{2,1,0:T(8,128)S(1)}, u32[]{:S(2)}, u32[]{:S(2)}) %collective-permute-start.5) | collective-permute-done | bytes 524320 | tf_op jit(solution)/shard_map/ppermute | solution.py:53
  447.0 4.2 subtract_select_fusion
  452.5 31.5 %all-reduce.16.cloned.1.call-done = f32[256,256]{0,1:T(8,128)} async-done(((f32[256,256]{0,1:T(8,128)}), f32[256,256]{0,1:T(8,128)}) %all-reduce.16.cloned.1.call-update) | async-done | bytes 262160 | tf_op jit(solution)/shard_map/psum | solution.py:17
  487.5 11.7 %cholesky.240 = f32[128,128]{1,0:T(8,128)S(1)} custom-call(f32[128,128]{1,0:T(8,128)S(1)} %cholesky.276), custom_call_target="Cholesky" | custom-call | tf_op jit(solution)/shard_map/jit(cholesky)/cholesky | solution.py:37
  500.0 10.4 %custom-call.19 = f32[1,128,128]{1,2,0:T(8,128)} custom-call(f32[1,128,128]{2,1,0:T(8,128)S(1)} %get-tuple-element.64), custom_call_target="InvertDiagBlocksLowerTriangular" | custom-call | tf_op jit(solution)/shard_map/jit(cholesky)/cholesky | solution.py:37
  514.0 11.7 %cholesky.257 = f32[128,128]{1,0:T(8,128)S(1)} custom-call(f32[128,128]{1,0:T(8,128)S(1)} %convolution_subtract_fusion.3), custom_call_target="Cholesky" | custom-call | tf_op jit(solution)/shard_map/jit(cholesky)/cholesky | solution.py:37
  529.0 5.9 while.8
  529.8 2.3 bitcast_dynamic-update-slice_fusion.8
  532.7 2.2 bitcast_dynamic-update-slice_fusion.8
  535.6 20.5 %custom-call.20 = f32[2,128,128]{1,2,0:T(8,128)S(1)} custom-call(f32[2,128,128]{2,1,0:T(8,128)} %copy-done.13), custom_call_target="InvertDiagBlocksLowerTriangular" | custom-call | tf_op jit(solution)/shard_map/triangular_solve/custom-call.0 | solution.py:38
  557.8 2.1 fusion
  559.9 78.4 %all-reduce.18.cloned.1.call-done = f32[4,256,256]{1,2,0:T(8,128)} async-done(((f32[4,256,256]{1,2,0:T(8,128)}), f32[4,256,256]{1,2,0:T(8,128)}) %all-reduce.18.cloned.1.call-update) | async-done | bytes 1048592 | tf_op jit(solution)/shard_map/psum | solution.py:17
  640.2 2.1 copy.37
  642.2 8.8 %collective-permute-done.6 = f32[2,256,256]{2,1,0:T(8,128)S(1)} collective-permute-done((f32[2,256,256]{2,1,0:T(8,128)}, f32[2,256,256]{2,1,0:T(8,128)S(1)}, u32[]{:S(2)}, u32[]{:S(2)}) %collective-permute-start.6) | collective-permute-done | bytes 524320 | tf_op jit(solution)/shard_map/ppermute | solution.py:53
  651.9 8.7 %collective-permute-done.7 = f32[2,256,256]{2,1,0:T(8,128)} collective-permute-done((f32[2,256,256]{2,1,0:T(8,128)S(1)}, f32[2,256,256]{2,1,0:T(8,128)}, u32[]{:S(2)}, u32[]{:S(2)}) %collective-permute-start.7) | collective-permute-done | bytes 524320 | tf_op jit(solution)/shard_map/ppermute | solution.py:53
  660.7 3.4 maximum_bitcast_fusion
  664.1 3.6 copy.42
  669.5 2.7 pad_maximum_fusion.2
  672.2 3.7 gather_fusion.2
  675.9 4.5 select_bitcast_fusion
  680.3 6.0 copy.41
  (137 shorter events, 50.7 us)
Async XLA Ops:
  7.2 40.5 %all-reduce.8.cloned.1.call-start = ((), (), s32[]{:S(2)}) async-start(), calls=%async_computation | async-start | bytes 524288 | tf_op jit(solution)/shard_map/psum | solution.py:17
  12.5 178.3 %all-reduce.10.cloned.1.call-start = ((), (), s32[]{:S(2)}) async-start(), calls=%async_computation.1 | async-start | bytes 2097152 | tf_op jit(solution)/shard_map/psum | solution.py:17
  112.4 149.4 %all-reduce.12.cloned.1.call-start = ((), (), s32[]{:S(2)}) async-start(), calls=%async_computation.2 | async-start | bytes 524288 | tf_op jit(solution)/shard_map/psum | solution.py:17
  192.1 8.7 %collective-permute-start = (f32[2,256,256]{2,1,0:T(8,128)S(1)}, f32[2,256,256]{2,1,0:T(8,128)S(1)}, u32[]{:S(2)}, u32[]{:S(2)}) collective-permute-start(f32[2,256,256]{2,1,0:T(8,128)S(1)} %bitcast.195), channel_id=1, source_target_pairs={{0,8},{8,16},{16,24},{24,0},{1,9},{9,17},{17,25},{25,1},{2,10},{10... | collective-permute-start | bytes 1572872 | tf_op jit(solution)/shard_map/ppermute | solution.py:53
  200.8 8.7 %collective-permute-start.1 = (f32[2,256,256]{2,1,0:T(8,128)S(1)}, f32[2,256,256]{2,1,0:T(8,128)}, u32[]{:S(2)}, u32[]{:S(2)}) collective-permute-start(f32[2,256,256]{2,1,0:T(8,128)S(1)} %collective-permute-done), channel_id=1, source_target_pairs={{0,8},{8,16},{16,24},{24,0},{1,9},{9,17},{17,25},{25,1},{2,10},{10... | collective-permute-start | bytes 1572872 | tf_op jit(solution)/shard_map/ppermute | solution.py:53
  209.5 8.8 %collective-permute-start.2 = (f32[2,256,256]{2,1,0:T(8,128)}, f32[2,256,256]{2,1,0:T(8,128)S(1)}, u32[]{:S(2)}, u32[]{:S(2)}) collective-permute-start(f32[2,256,256]{2,1,0:T(8,128)} %collective-permute-done.1), channel_id=1, source_target_pairs={{0,8},{8,16},{16,24},{24,0},{1,9},{9,17},{17,25},{25,1},{2,10},{10... | collective-permute-start | bytes 1572872 | tf_op jit(solution)/shard_map/ppermute | solution.py:53
  220.8 3.7 copy-start.2
  227.7 1.3 copy-start
  229.8 185.5 %all-reduce.14.cloned.1.call-start = ((), (), s32[]{:S(2)}) async-start(), calls=%async_computation.3 | async-start | bytes 2097152 | tf_op jit(solution)/shard_map/psum | solution.py:17
  263.9 0.7 copy-start.6
  264.6 70.2 %copy-start.1 = (f32[4,256,2,256]{1,3,2,0:T(8,128)S(1)}, f32[4,256,2,256]{1,3,2,0:T(8,128)}, u32[]{:S(2)}) copy-start(f32[4,256,2,256]{1,3,2,0:T(8,128)} %copy-done) | copy-start | bytes 6291460
  311.9 0.7 copy-start.14
  336.9 147.1 %all-reduce.16.cloned.1.call-start = ((), (), s32[]{:S(2)}) async-start(), calls=%async_computation.4 | async-start | bytes 524288 | tf_op jit(solution)/shard_map/psum | solution.py:17
  416.6 25.9 %copy-start.5 = (f32[2,1,256,256]{3,2,0,1:T(8,128)}, f32[2,1,256,256]{3,2,0,1:T(8,128)S(1)}, u32[]{:S(2)}) copy-start(f32[2,1,256,256]{3,2,0,1:T(8,128)S(1)} %copy.30) | copy-start | bytes 1572868
  416.6 8.7 %collective-permute-start.3 = (f32[2,256,256]{2,1,0:T(8,128)S(1)}, f32[2,256,256]{2,1,0:T(8,128)S(1)}, u32[]{:S(2)}, u32[]{:S(2)}) collective-permute-start(f32[2,256,256]{2,1,0:T(8,128)S(1)} %bitcast.199), channel_id=1, source_target_pairs={{0,8},{8,16},{16,24},{24,0},{1,9},{9,17},{17,25},{25,1},{2,10},{10... | collective-permute-start | bytes 1572872 | tf_op jit(solution)/shard_map/ppermute | solution.py:53
  425.2 17.2 %copy-start.10 = (f32[2,256,256]{2,1,0:T(8,128)}, f32[2,256,256]{2,1,0:T(8,128)S(1)}, u32[]{:S(2)}) copy-start(f32[2,256,256]{2,1,0:T(8,128)S(1)} %collective-permute-done.3) | copy-start | bytes 1572868
  425.2 8.6 %collective-permute-start.4 = (f32[2,256,256]{2,1,0:T(8,128)S(1)}, f32[2,256,256]{2,1,0:T(8,128)S(1)}, u32[]{:S(2)}, u32[]{:S(2)}) collective-permute-start(f32[2,256,256]{2,1,0:T(8,128)S(1)} %collective-permute-done.3), channel_id=1, source_target_pairs={{0,8},{8,16},{16,24},{24,0},{1,9},{9,17},{17,25},{25,1},{2,10},{10... | collective-permute-start | bytes 1572872 | tf_op jit(solution)/shard_map/ppermute | solution.py:53
  433.8 8.6 %copy-start.11 = (f32[2,256,256]{2,1,0:T(8,128)}, f32[2,256,256]{2,1,0:T(8,128)S(1)}, u32[]{:S(2)}) copy-start(f32[2,256,256]{2,1,0:T(8,128)S(1)} %collective-permute-done.4) | copy-start | bytes 1572868
  433.8 8.6 %collective-permute-start.5 = (f32[2,256,256]{2,1,0:T(8,128)S(1)}, f32[2,256,256]{2,1,0:T(8,128)S(1)}, u32[]{:S(2)}, u32[]{:S(2)}) collective-permute-start(f32[2,256,256]{2,1,0:T(8,128)S(1)} %collective-permute-done.4), channel_id=1, source_target_pairs={{0,8},{8,16},{16,24},{24,0},{1,9},{9,17},{17,25},{25,1},{2,10},{10... | collective-permute-start | bytes 1572872 | tf_op jit(solution)/shard_map/ppermute | solution.py:53
  442.5 0.8 copy-start.12
  451.9 186.4 %all-reduce.18.cloned.1.call-start = ((), (), s32[]{:S(2)}) async-start(), calls=%async_computation.5 | async-start | bytes 2097152 | tf_op jit(solution)/shard_map/psum | solution.py:17
  486.8 0.7 copy-start.7
  534.9 0.7 copy-start.13
  642.2 8.8 %collective-permute-start.6 = (f32[2,256,256]{2,1,0:T(8,128)}, f32[2,256,256]{2,1,0:T(8,128)S(1)}, u32[]{:S(2)}, u32[]{:S(2)}) collective-permute-start(f32[2,256,256]{2,1,0:T(8,128)} %bitcast.197), channel_id=1, source_target_pairs={{0,8},{8,16},{16,24},{24,0},{1,9},{9,17},{17,25},{25,1},{2,10},{10... | collective-permute-start | bytes 1572872 | tf_op jit(solution)/shard_map/ppermute | solution.py:53
  651.1 0.8 copy-start.8
  651.9 8.7 %collective-permute-start.7 = (f32[2,256,256]{2,1,0:T(8,128)S(1)}, f32[2,256,256]{2,1,0:T(8,128)}, u32[]{:S(2)}, u32[]{:S(2)}) collective-permute-start(f32[2,256,256]{2,1,0:T(8,128)S(1)} %collective-permute-done.6), channel_id=1, source_target_pairs={{0,8},{8,16},{16,24},{24,0},{1,9},{9,17},{17,25},{25,1},{2,10},{10... | collective-permute-start | bytes 1572872 | tf_op jit(solution)/shard_map/ppermute | solution.py:53
  660.6 8.9 %collective-permute-start.8 = (f32[2,256,256]{2,1,0:T(8,128)}, f32[2,256,256]{2,1,0:T(8,128)}, u32[]{:S(2)}, u32[]{:S(2)}) collective-permute-start(f32[2,256,256]{2,1,0:T(8,128)} %collective-permute-done.7), channel_id=1, source_target_pairs={{0,8},{8,16},{16,24},{24,0},{1,9},{9,17},{17,25},{25,1},{2,10},{10... | collective-permute-start | bytes 1572872 | tf_op jit(solution)/shard_map/ppermute | solution.py:53
  664.1 5.4 copy-start.4
  664.1 5.4 copy-start.9
  672.2 3.7 copy-start.3
Sparse Core Ops, SparseCore 0:
  12.7 34.9 all-reduce.7
  112.5 78.2 all-reduce.9
  229.9 31.8 all-reduce.11
  337.0 78.2 all-reduce.13
  452.0 31.8 all-reduce.15
  560.0 78.2 all-reduce.17
